TPU v7x, 32 devices: a whole 2x2x4 slice. The times are simulated.
32 devices in a mesh: layer: 4 (over y, x), row: 2 (over core), col: 4 (over z).
Axes of the slice: x: 2, y: 2, z: 4, core: 2. Of those that a mesh axis runs over, the one named last changes fastest.
Arguments:
- cols: int32 [64, 16], P(('row', 'col'), 'layer'), may hold values from -1 to 63, as said below
- vals: bfloat16 [64, 16, 256, 256], P(('row', 'col'), 'layer'), as said below
- outcols: int32 [64, 4], P(('row', 'col')), may hold values from -1 to 63, as said below
Outputs:
- purified: bfloat16 [64, 4, 256, 256], P(('row', 'col'), 'layer')
Inputs may be any that keep to these rules, and one draw needn't show every extreme that they name: `cols`: slots 4 * l to 4 * l + 3 of block row i hold distinct block columns k with k mod 4 = l and |k - i| <= 6, or -1. Column i is always listed in row i, and k is listed in row i exactly when i is listed in row k. vals[i, s] is block (i, cols[i, s]) of a symmetric matrix: the block listed at (k, i) is the transpose of the one at (i, k). Slots holding -1 hold zeros. `outcols`: block row i lists distinct block columns j with i <= j <= i + 12, always i itself, or -1.
All inputs are finite; a program needn't handle non-finite values.
Results may differ from a plain program's by a relative error of at most 0.0085.
Values may be sent and summed in bfloat16 or wider, within the bound.
A program may use at most 64 MiB of HBM per device.

v0:
```python
import jax
import jax.numpy as jnp
from jax import lax
from jax.sharding import PartitionSpec as P

W = 6


def passed_along(value, axis, by):
    peers = lax.axis_size(axis)
    pairs = [(i, i + by) for i in range(peers) if 0 <= i + by < peers]
    return lax.ppermute(value, axis, pairs)


def per_device(cols, vals, outcols):
    rows = vals.shape[0]
    need = 2 * W
    hops = -(-need // rows)
    blocks_list = [vals]
    column_list = [cols]
    send_blocks = vals
    send_cols = cols
    for hop in range(1, hops + 1):
        count = min(rows, need - (hop - 1) * rows)
        got_blocks, got_cols = passed_along(
            (send_blocks[:count], send_cols[:count]), ("row", "col"), -1
        )
        blocks_list.append(got_blocks)
        column_list.append(got_cols)
        send_blocks = got_blocks
        send_cols = got_cols
    extended = jnp.concatenate(blocks_list, axis=0)
    extended_cols = jnp.concatenate(column_list, axis=0)
    offset_rows = lax.axis_index(("row", "col")) * rows

    def one_row(inputs):
        left, left_cols, targets = inputs
        where = jnp.clip(targets - offset_rows, 0, extended_cols.shape[0] - 1)
        right = extended[where]
        right_cols = extended_cols[where]
        hits = (
            (left_cols[None, :, None] == right_cols[:, None, :]) & (left_cols[None, :, None] >= 0)
        ).astype(jnp.bfloat16)
        moved = jnp.einsum(
            "ost,otab->osab", hits, right, preferred_element_type=jnp.float32
        ).astype(jnp.bfloat16)
        product = jnp.einsum("sab,oscb->oac", left, moved, preferred_element_type=jnp.float32)
        owned = (left_cols[None, :] == targets[:, None]).astype(jnp.bfloat16)
        twice = 2.0 * jnp.einsum("os,sab->oab", owned, left, preferred_element_type=jnp.float32)
        return jnp.where(targets[:, None, None] >= 0, twice - product, jnp.float32(0.0))

    partials = lax.map(one_row, (vals, cols, outcols))
    total = lax.psum(partials.astype(jnp.bfloat16), "layer").astype(jnp.float32)
    share = outcols.shape[1] // lax.axis_size("layer")
    mine = lax.dynamic_slice_in_dim(total, lax.axis_index("layer") * share, share, 1)
    return mine.astype(jnp.bfloat16)


def solution(mesh):
    in_specs = (
        P(("row", "col"), "layer"),
        P(("row", "col"), "layer", None, None),
        P(("row", "col"), None),
    )
    out_specs = P(("row", "col"), "layer", None, None)
    return jax.shard_map(
        per_device, mesh=mesh, in_specs=in_specs, out_specs=out_specs, check_vma=False
    )
```

profile of v0, /device:TPU:0, one launch (start us, length us, event | category | flops | bytes accessed | tf_op | source)
XLA Modules:
  0.0 372.5 jit_solution(15405082629851489519)
XLA Ops:
  6.5 1.4 collective-permute-start.2
  8.0 94.4 %collective-permute-done.2 = bf16[8,4,256,256]{3,2,1,0:T(8,128)(2,1)S(1)} collective-permute-done((bf16[8,4,256,256]{3,2,1,0:T(8,128)(2,1)}, bf16[8,4,256,256]{3,2,1,0:T(8,128)(2,1)S(1)}, u32[]{:S(2)}, u32[]{:S(2)}) %collective-permute-start.2) | collective-permute-done | bytes 4194336 | tf_op jit(solution)/shard_map/ppermute | solution.py:12
  102.4 2.0 copy-done
  104.4 1.5 slice.12
  105.9 1.3 collective-permute-start.3
  107.2 1.3 collective-permute-start
  108.6 46.2 %collective-permute-done = s32[8,4]{0,1:T(4,128)S(1)} collective-permute-done((s32[8,4]{0,1:T(4,128)S(1)}, s32[8,4]{0,1:T(4,128)S(1)}, u32[]{:S(2)}, u32[]{:S(2)}) %collective-permute-start) | collective-permute-done | bytes 160 | tf_op jit(solution)/shard_map/ppermute | solution.py:12
  154.8 1.3 collective-permute-start.1
  156.1 4.2 %collective-permute-done.1 = s32[4,4]{0,1:T(4,128)S(1)} collective-permute-done((s32[4,4]{0,1:T(4,128)S(1)}, s32[4,4]{0,1:T(4,128)S(1)}, u32[]{:S(2)}, u32[]{:S(2)}) %collective-permute-start.1) | collective-permute-done | bytes 96 | tf_op jit(solution)/shard_map/ppermute | solution.py:12
  160.4 8.8 %pad_maximum_fusion = bf16[20,4,256,256]{3,2,1,0:T(8,128)(2,1)} fusion(bf16[4,4,256,256]{3,2,1,0:T(8,128)(2,1)S(1)} %collective-permute-done.3, bf16[8,4,256,256]{3,2,1,0:T(8,128)(2,1)} %copy-done, bf16[8,4,256,256]{3,2,1,0:T(8,128)(2,1)} %param.6), kind=kLoop, calls=%fused_computation.35 | loop fusion | flops 10485760 | bytes 20971520 | tf_op jit(solution)/shard_map/concatenate | solution.py:32
  169.2 90.0 %while.10 = (s32[]{:T(128)}, bf16[8,4,256,256]{3,2,1,0:T(8,128)(2,1)}, s32[8,4]{1,0:T(8,128)S(1)}, s32[8,4]{1,0:T(8,128)S(1)}, bf16[8,4,256,256]{3,2,1,0:T(8,128...) while((s32[]{:T(128)}, bf16[8,4,256,256]{3,2,1,0:T(8,128)(2,1)}, ...), condition=%wide.region_1.2_spmd, body=%wide.region_0.1_spmd.sunk | while | flops 548144256 | bytes 19403772 | solution.py:52
  169.2 4.7 %gather_fusion = bf16[4,4,256,256]{3,2,1,0:T(8,128)(2,1)S(1)} fusion(bf16[20,4,256,256]{3,2,1,0:T(8,128)(2,1)} %get-tuple-element.168, s32[1024]{0:T(1024)S(1)} %pad_clamp_fusion.2), kind=kCustom, calls=%fused_computation.1.clone.1 | custom fusion | bytes 4194320 | tf_op jit(solution)/shard_map/while/body/eval_jaxpr/gather | solution.py:39
  174.5 1.8 fusion.37
  176.2 1.1 constant_dynamic-slice_fusion.4
  177.7 0.8 fusion.38
  179.6 0.9 copy_dynamic-update-slice_fusion.2
  180.5 4.7 %gather_fusion = bf16[4,4,256,256]{3,2,1,0:T(8,128)(2,1)S(1)} fusion(bf16[20,4,256,256]{3,2,1,0:T(8,128)(2,1)} %get-tuple-element.168, s32[1024]{0:T(1024)S(1)} %pad_clamp_fusion.2), kind=kCustom, calls=%fused_computation.1.clone.1 | custom fusion | bytes 4194320 | tf_op jit(solution)/shard_map/while/body/eval_jaxpr/gather | solution.py:39
  185.7 1.8 fusion.37
  187.5 1.1 constant_dynamic-slice_fusion.4
  189.0 0.8 fusion.38
  190.8 0.9 copy_dynamic-update-slice_fusion.2
  191.7 4.7 %gather_fusion = bf16[4,4,256,256]{3,2,1,0:T(8,128)(2,1)S(1)} fusion(bf16[20,4,256,256]{3,2,1,0:T(8,128)(2,1)} %get-tuple-element.168, s32[1024]{0:T(1024)S(1)} %pad_clamp_fusion.2), kind=kCustom, calls=%fused_computation.1.clone.1 | custom fusion | bytes 4194320 | tf_op jit(solution)/shard_map/while/body/eval_jaxpr/gather | solution.py:39
  197.0 1.8 fusion.37
  198.7 1.1 constant_dynamic-slice_fusion.4
  202.1 0.9 copy_dynamic-update-slice_fusion.2
  203.0 4.7 %gather_fusion = bf16[4,4,256,256]{3,2,1,0:T(8,128)(2,1)S(1)} fusion(bf16[20,4,256,256]{3,2,1,0:T(8,128)(2,1)} %get-tuple-element.168, s32[1024]{0:T(1024)S(1)} %pad_clamp_fusion.2), kind=kCustom, calls=%fused_computation.1.clone.1 | custom fusion | bytes 4194320 | tf_op jit(solution)/shard_map/while/body/eval_jaxpr/gather | solution.py:39
  208.2 1.8 fusion.37
  210.0 1.1 constant_dynamic-slice_fusion.4
  213.3 0.9 copy_dynamic-update-slice_fusion.2
  214.2 4.7 %gather_fusion = bf16[4,4,256,256]{3,2,1,0:T(8,128)(2,1)S(1)} fusion(bf16[20,4,256,256]{3,2,1,0:T(8,128)(2,1)} %get-tuple-element.168, s32[1024]{0:T(1024)S(1)} %pad_clamp_fusion.2), kind=kCustom, calls=%fused_computation.1.clone.1 | custom fusion | bytes 4194320 | tf_op jit(solution)/shard_map/while/body/eval_jaxpr/gather | solution.py:39
  219.5 1.8 fusion.37
  221.2 1.1 constant_dynamic-slice_fusion.4
  222.7 0.8 fusion.38
  224.6 0.9 copy_dynamic-update-slice_fusion.2
  225.5 4.7 %gather_fusion = bf16[4,4,256,256]{3,2,1,0:T(8,128)(2,1)S(1)} fusion(bf16[20,4,256,256]{3,2,1,0:T(8,128)(2,1)} %get-tuple-element.168, s32[1024]{0:T(1024)S(1)} %pad_clamp_fusion.2), kind=kCustom, calls=%fused_computation.1.clone.1 | custom fusion | bytes 4194320 | tf_op jit(solution)/shard_map/while/body/eval_jaxpr/gather | solution.py:39
  230.7 1.8 fusion.37
  232.5 1.1 constant_dynamic-slice_fusion.4
  235.8 0.9 copy_dynamic-update-slice_fusion.2
  236.8 4.7 %gather_fusion = bf16[4,4,256,256]{3,2,1,0:T(8,128)(2,1)S(1)} fusion(bf16[20,4,256,256]{3,2,1,0:T(8,128)(2,1)} %get-tuple-element.168, s32[1024]{0:T(1024)S(1)} %pad_clamp_fusion.2), kind=kCustom, calls=%fused_computation.1.clone.1 | custom fusion | bytes 4194320 | tf_op jit(solution)/shard_map/while/body/eval_jaxpr/gather | solution.py:39
  242.0 1.8 fusion.37
  243.8 1.1 constant_dynamic-slice_fusion.4
  247.1 0.9 copy_dynamic-update-slice_fusion.2
  248.0 4.7 %gather_fusion = bf16[4,4,256,256]{3,2,1,0:T(8,128)(2,1)S(1)} fusion(bf16[20,4,256,256]{3,2,1,0:T(8,128)(2,1)} %get-tuple-element.168, s32[1024]{0:T(1024)S(1)} %pad_clamp_fusion.2), kind=kCustom, calls=%fused_computation.1.clone.1 | custom fusion | bytes 4194320 | tf_op jit(solution)/shard_map/while/body/eval_jaxpr/gather | solution.py:39
  253.2 1.8 fusion.37
  255.0 1.1 constant_dynamic-slice_fusion.4
  258.4 0.9 copy_dynamic-update-slice_fusion.2
  259.2 104.2 %all-reduce.2.cloned.1.call-done = bf16[8,4,256,256]{3,2,1,0:T(8,128)(2,1)} async-done(((bf16[8,4,256,256]{3,2,1,0:T(8,128)(2,1)}), bf16[8,4,256,256]{3,2,1,0:T(8,128)(2,1)}) %all-reduce.2.cloned.1.call-update) | async-done | bytes 4194320 | tf_op jit(solution)/shard_map/psum | solution.py:53
  363.4 2.3 convert_convert_fusion
  (74 shorter events, 20.6 us)
Async XLA Ops:
  6.5 100.6 %copy-start.1 = (s32[8,4]{0,1:T(4,128)S(1)}, s32[8,4]{0,1:T(4,128)}, u32[]{:S(2)}) copy-start(s32[8,4]{0,1:T(4,128)} %param.5) | copy-start | bytes 388
  6.5 102.0 %copy-start.2 = (s32[8,4]{0,1:T(4,128)S(1)}, s32[8,4]{0,1:T(4,128)}, u32[]{:S(2)}) copy-start(s32[8,4]{0,1:T(4,128)} %param.7) | copy-start | bytes 388
  6.5 356.9 %all-reduce.2.cloned.1.call-start = ((), (), s32[]{:S(2)}) async-start(), calls=%async_computation | async-start | bytes 8388608 | tf_op jit(solution)/shard_map/psum | solution.py:53
  6.5 95.9 %collective-permute-start.2 = (bf16[8,4,256,256]{3,2,1,0:T(8,128)(2,1)}, bf16[8,4,256,256]{3,2,1,0:T(8,128)(2,1)S(1)}, u32[]{:S(2)}, u32[]{:S(2)}) collective-permute-start(bf16[8,4,256,256]{3,2,1,0:T(8,128)(2,1)} %param.6), channel_id=1, source_target_pairs={{1,0},{2,1},{3,2},{4,3},{5,4},{6,5},{7,6},{9,8},{10,9},{11,10},{12... | collective-permute-start | bytes 12582920 | tf_op jit(solution)/shard_map/ppermute | solution.py:12
  102.4 2.0 copy-start
  105.9 54.6 %collective-permute-start.3 = (bf16[4,4,256,256]{3,2,1,0:T(8,128)(2,1)}, bf16[4,4,256,256]{3,2,1,0:T(8,128)(2,1)S(1)}, u32[]{:S(2)}, u32[]{:S(2)}) collective-permute-start(bf16[4,4,256,256]{3,2,1,0:T(8,128)(2,1)} %slice.12), channel_id=1, source_target_pairs={{1,0},{2,1},{3,2},{4,3},{5,4},{6,5},{7,6},{9,8},{10,9},{11,10},{12... | collective-permute-start | bytes 6291464 | tf_op jit(solution)/shard_map/ppermute | solution.py:12
  107.2 47.6 %collective-permute-start = (s32[8,4]{0,1:T(4,128)S(1)}, s32[8,4]{0,1:T(4,128)S(1)}, u32[]{:S(2)}, u32[]{:S(2)}) collective-permute-start(s32[8,4]{0,1:T(4,128)S(1)} %copy-done.1), channel_id=1, source_target_pairs={{1,0},{2,1},{3,2},{4,3},{5,4},{6,5},{7,6},{9,8},{10,9},{11,10},{12... | collective-permute-start | bytes 392 | tf_op jit(solution)/shard_map/ppermute | solution.py:12
  154.8 5.5 %collective-permute-start.1 = (s32[4,4]{0,1:T(4,128)S(1)}, s32[4,4]{0,1:T(4,128)S(1)}, u32[]{:S(2)}, u32[]{:S(2)}) collective-permute-start(s32[4,4]{0,1:T(4,128)S(1)} %bitcast.54), channel_id=1, source_target_pairs={{1,0},{2,1},{3,2},{4,3},{5,4},{6,5},{7,6},{9,8},{10,9},{11,10},{12... | collective-permute-start | bytes 200 | tf_op jit(solution)/shard_map/ppermute | solution.py:12
Sparse Core Ops, SparseCore 0:
  259.4 103.9 all-reduce.1
where the time goes:
time: 374 us; the launch traced here: 373 us
  waiting for transfers between devices  249 us (67%)
  local copies, waits for them, and re-layouts  67.6 us (18%)
  matrix products  25.5 us (7%)
  between operations  13.5 us (4%)
  other arithmetic  11.3 us (3%)
  starting transfers between devices  5.27 us (1%)
    ppermute x4, waiting for transfers between devices, passed_along(): return lax.ppermute(value, axis, pairs)  145 us
    psum x1, waiting for transfers between devices, per_device(): total = lax.psum(partials.astype(jnp.bfloat16), 'layer').astype(jnp.float32)  104 us
    gather x8, local copies, waits for them, and re-layouts, one_row(): right = extended[where]  37.3 us
    dot_general x8, matrix products, one_row(): jnp.einsum('ost,otab->osab', hits, right, preferred_element_type=jnp.floa...  14.1 us
    dynamic_slice x16, local copies, waits for them, and re-layouts, per_device(): partials = lax.map(one_row, (vals, cols, outcols))  11.9 us
    concatenate x1, other arithmetic, per_device(): extended = jnp.concatenate(blocks_list, axis=0)  8.76 us
  transfers between devices with their start and end apart: 5, of which 4 were waited for; matrix products, arithmetic and copies ran while one was open for 0% of the time, Pallas kernels for 0%

commit v1 on v0

--- a/solution.py
+++ b/solution.py
@@ -50,7 +50,9 @@
         return jnp.where(targets[:, None, None] >= 0, twice - product, jnp.float32(0.0))
 
     partials = lax.map(one_row, (vals, cols, outcols))
-    total = lax.psum(partials.astype(jnp.bfloat16), "layer").astype(jnp.float32)
+    total = jnp.sum(lax.all_gather(partials.astype(jnp.bfloat16), "layer"), axis=0).astype(
+        jnp.float32
+    )
     share = outcols.shape[1] // lax.axis_size("layer")
     mine = lax.dynamic_slice_in_dim(total, lax.axis_index("layer") * share, share, 1)
     return mine.astype(jnp.bfloat16)

time: 374 us -> 439 us (1.17)
  waiting for transfers between devices: 249 us -> 303 us
  other arithmetic: 11.3 us -> 23 us
    all_gather x0 -> x1, waiting for transfers between devices: none -> 158 us  [per_device(): lax.all_gather(partials.astype(jnp.bfloat16), 'layer')]
    psum x1 -> x0, waiting for transfers between devices: 104 us -> none  [per_device(): total = lax.psum(partials.astype(jnp.bfloat16), 'layer').astype(jnp.float32)]
    reduce_sum x0 -> x1, other arithmetic: none -> 11.7 us  [per_device(): jnp.sum(lax.all_gather(partials.astype(jnp.bfloat16), 'layer'), axis=0)]
where the time goes in v1:
time: 439 us; the launch traced here: 438 us
  waiting for transfers between devices  303 us (69%)
  local copies, waits for them, and re-layouts  67.5 us (15%)
  matrix products  25.5 us (6%)
  other arithmetic  23 us (5%)
  between operations  13.5 us (3%)
  starting transfers between devices  5.27 us (1%)
    all_gather x1, waiting for transfers between devices, per_device(): lax.all_gather(partials.astype(jnp.bfloat16), 'layer')  158 us
    ppermute x4, waiting for transfers between devices, passed_along(): return lax.ppermute(value, axis, pairs)  145 us
    gather x8, local copies, waits for them, and re-layouts, one_row(): right = extended[where]  37.3 us
    dot_general x8, matrix products, one_row(): jnp.einsum('ost,otab->osab', hits, right, preferred_element_type=jnp.floa...  14.1 us
    dynamic_slice x16, local copies, waits for them, and re-layouts, per_device(): partials = lax.map(one_row, (vals, cols, outcols))  11.9 us
    reduce_sum x1, other arithmetic, per_device(): jnp.sum(lax.all_gather(partials.astype(jnp.bfloat16), 'layer'), axis=0)  11.7 us
  transfers between devices with their start and end apart: 5, of which 4 were waited for; matrix products, arithmetic and copies ran while one was open for 0% of the time, Pallas kernels for 0%

profile of v1, /device:TPU:0, one launch (start us, length us, event | category | flops | bytes accessed | tf_op | source)
XLA Modules:
  0.0 437.9 jit_solution(13494350730903349229)
XLA Ops:
  6.5 1.4 collective-permute-start.2
  8.0 94.4 %collective-permute-done.2 = bf16[8,4,256,256]{3,2,1,0:T(8,128)(2,1)S(1)} collective-permute-done((bf16[8,4,256,256]{3,2,1,0:T(8,128)(2,1)}, bf16[8,4,256,256]{3,2,1,0:T(8,128)(2,1)S(1)}, u32[]{:S(2)}, u32[]{:S(2)}) %collective-permute-start.2) | collective-permute-done | bytes 4194336 | tf_op jit(solution)/shard_map/ppermute | solution.py:12
  102.4 2.0 copy-done
  104.4 1.5 slice.12
  105.8 1.3 collective-permute-start.3
  107.1 1.3 collective-permute-start
  108.6 46.2 %collective-permute-done = s32[8,4]{0,1:T(4,128)S(1)} collective-permute-done((s32[8,4]{0,1:T(4,128)S(1)}, s32[8,4]{0,1:T(4,128)S(1)}, u32[]{:S(2)}, u32[]{:S(2)}) %collective-permute-start) | collective-permute-done | bytes 160 | tf_op jit(solution)/shard_map/ppermute | solution.py:12
  154.8 1.3 collective-permute-start.1
  156.1 4.2 collective-permute-done.1
  160.4 8.8 %pad_maximum_fusion = bf16[20,4,256,256]{3,2,1,0:T(8,128)(2,1)} fusion(bf16[4,4,256,256]{3,2,1,0:T(8,128)(2,1)S(1)} %collective-permute-done.3, bf16[8,4,256,256]{3,2,1,0:T(8,128)(2,1)} %copy-done, bf16[8,4,256,256]{3,2,1,0:T(8,128)(2,1)} %param.6), kind=kLoop, calls=%fused_computation.35 | loop fusion | flops 10485760 | bytes 20971520 | tf_op jit(solution)/shard_map/concatenate | solution.py:32
  169.2 90.0 %while.10 = (s32[]{:T(128)}, bf16[8,4,256,256]{3,2,1,0:T(8,128)(2,1)}, s32[8,4]{1,0:T(8,128)S(1)}, s32[8,4]{1,0:T(8,128)S(1)}, bf16[8,4,256,256]{3,2,1,0:T(8,128...) while((s32[]{:T(128)}, bf16[8,4,256,256]{3,2,1,0:T(8,128)(2,1)}, ...), condition=%wide.region_1.2_spmd, body=%wide.region_0.1_spmd.sunk | while | flops 548144256 | bytes 19403772 | solution.py:52
  169.2 4.7 %gather_fusion = bf16[4,4,256,256]{3,2,1,0:T(8,128)(2,1)S(1)} fusion(bf16[20,4,256,256]{3,2,1,0:T(8,128)(2,1)} %get-tuple-element.168, s32[1024]{0:T(1024)S(1)} %pad_clamp_fusion.2), kind=kCustom, calls=%fused_computation.1.clone.1 | custom fusion | bytes 4194320 | tf_op jit(solution)/shard_map/while/body/eval_jaxpr/gather | solution.py:39
  174.5 1.8 fusion.37
  176.2 1.1 constant_dynamic-slice_fusion.4
  179.6 0.9 copy_dynamic-update-slice_fusion.2
  180.5 4.7 %gather_fusion = bf16[4,4,256,256]{3,2,1,0:T(8,128)(2,1)S(1)} fusion(bf16[20,4,256,256]{3,2,1,0:T(8,128)(2,1)} %get-tuple-element.168, s32[1024]{0:T(1024)S(1)} %pad_clamp_fusion.2), kind=kCustom, calls=%fused_computation.1.clone.1 | custom fusion | bytes 4194320 | tf_op jit(solution)/shard_map/while/body/eval_jaxpr/gather | solution.py:39
  185.7 1.8 fusion.37
  187.5 1.1 constant_dynamic-slice_fusion.4
  189.0 0.8 fusion.38
  190.8 0.9 copy_dynamic-update-slice_fusion.2
  191.7 4.7 %gather_fusion = bf16[4,4,256,256]{3,2,1,0:T(8,128)(2,1)S(1)} fusion(bf16[20,4,256,256]{3,2,1,0:T(8,128)(2,1)} %get-tuple-element.168, s32[1024]{0:T(1024)S(1)} %pad_clamp_fusion.2), kind=kCustom, calls=%fused_computation.1.clone.1 | custom fusion | bytes 4194320 | tf_op jit(solution)/shard_map/while/body/eval_jaxpr/gather | solution.py:39
  196.9 1.8 fusion.37
  198.7 1.1 constant_dynamic-slice_fusion.4
  202.1 0.9 copy_dynamic-update-slice_fusion.2
  203.0 4.7 %gather_fusion = bf16[4,4,256,256]{3,2,1,0:T(8,128)(2,1)S(1)} fusion(bf16[20,4,256,256]{3,2,1,0:T(8,128)(2,1)} %get-tuple-element.168, s32[1024]{0:T(1024)S(1)} %pad_clamp_fusion.2), kind=kCustom, calls=%fused_computation.1.clone.1 | custom fusion | bytes 4194320 | tf_op jit(solution)/shard_map/while/body/eval_jaxpr/gather | solution.py:39
  208.2 1.8 fusion.37
  210.0 1.1 constant_dynamic-slice_fusion.4
  213.3 0.9 copy_dynamic-update-slice_fusion.2
  214.2 4.7 %gather_fusion = bf16[4,4,256,256]{3,2,1,0:T(8,128)(2,1)S(1)} fusion(bf16[20,4,256,256]{3,2,1,0:T(8,128)(2,1)} %get-tuple-element.168, s32[1024]{0:T(1024)S(1)} %pad_clamp_fusion.2), kind=kCustom, calls=%fused_computation.1.clone.1 | custom fusion | bytes 4194320 | tf_op jit(solution)/shard_map/while/body/eval_jaxpr/gather | solution.py:39
  219.5 1.8 fusion.37
  221.2 1.1 constant_dynamic-slice_fusion.4
  224.6 0.9 copy_dynamic-update-slice_fusion.2
  225.5 4.7 %gather_fusion = bf16[4,4,256,256]{3,2,1,0:T(8,128)(2,1)S(1)} fusion(bf16[20,4,256,256]{3,2,1,0:T(8,128)(2,1)} %get-tuple-element.168, s32[1024]{0:T(1024)S(1)} %pad_clamp_fusion.2), kind=kCustom, calls=%fused_computation.1.clone.1 | custom fusion | bytes 4194320 | tf_op jit(solution)/shard_map/while/body/eval_jaxpr/gather | solution.py:39
  230.7 1.8 fusion.37
  232.5 1.1 constant_dynamic-slice_fusion.4
  235.8 0.9 copy_dynamic-update-slice_fusion.2
  236.7 4.7 %gather_fusion = bf16[4,4,256,256]{3,2,1,0:T(8,128)(2,1)S(1)} fusion(bf16[20,4,256,256]{3,2,1,0:T(8,128)(2,1)} %get-tuple-element.168, s32[1024]{0:T(1024)S(1)} %pad_clamp_fusion.2), kind=kCustom, calls=%fused_computation.1.clone.1 | custom fusion | bytes 4194320 | tf_op jit(solution)/shard_map/while/body/eval_jaxpr/gather | solution.py:39
  242.0 1.8 fusion.37
  243.7 1.1 constant_dynamic-slice_fusion.4
  247.1 0.9 copy_dynamic-update-slice_fusion.2
  248.0 4.7 %gather_fusion = bf16[4,4,256,256]{3,2,1,0:T(8,128)(2,1)S(1)} fusion(bf16[20,4,256,256]{3,2,1,0:T(8,128)(2,1)} %get-tuple-element.168, s32[1024]{0:T(1024)S(1)} %pad_clamp_fusion.2), kind=kCustom, calls=%fused_computation.1.clone.1 | custom fusion | bytes 4194320 | tf_op jit(solution)/shard_map/while/body/eval_jaxpr/gather | solution.py:39
  253.2 1.8 fusion.37
  255.0 1.1 constant_dynamic-slice_fusion.4
  256.5 0.8 fusion.38
  258.3 0.9 copy_dynamic-update-slice_fusion.2
  259.2 157.8 %all-gather.3.cloned.1.call-done = bf16[32,4,256,256]{3,2,1,0:T(8,128)(2,1)} async-done(((bf16[8,4,256,256]{3,2,1,0:T(8,128)(2,1)}), bf16[32,4,256,256]{3,2,1,0:T(8,128)(2,1)}) %all-gather.3.cloned.1.call-update) | async-done | bytes 16777232 | tf_op jit(solution)/shard_map/all_gather | solution.py:53
  417.1 11.7 %reduce_sum.12 = bf16[8,4,256,256]{3,2,1,0:T(8,128)(2,1)} reduce(bf16[4,8,4,256,256]{4,3,2,1,0:T(8,128)(2,1)} %bitcast.54, bf16[]{:T(256)} %constant.46.clone.1), dimensions={0}, to_apply=%region_2.3 | reduce | flops 6291456 | bytes 20971522 | tf_op jit(solution)/shard_map/reduce_sum | solution.py:53
  428.8 2.3 convert_convert_fusion
  (75 shorter events, 21.3 us)
Async XLA Ops:
  6.5 100.6 %copy-start.1 = (s32[8,4]{0,1:T(4,128)S(1)}, s32[8,4]{0,1:T(4,128)}, u32[]{:S(2)}) copy-start(s32[8,4]{0,1:T(4,128)} %param.5) | copy-start | bytes 388
  6.5 102.0 %copy-start.2 = (s32[8,4]{0,1:T(4,128)S(1)}, s32[8,4]{0,1:T(4,128)}, u32[]{:S(2)}) copy-start(s32[8,4]{0,1:T(4,128)} %param.7) | copy-start | bytes 388
  6.5 410.5 %all-gather.3.cloned.1.call-start = ((), (), s32[]{:S(2)}) async-start(), calls=%async_computation | async-start | bytes 20971520 | tf_op jit(solution)/shard_map/all_gather | solution.py:53
  6.5 95.9 %collective-permute-start.2 = (bf16[8,4,256,256]{3,2,1,0:T(8,128)(2,1)}, bf16[8,4,256,256]{3,2,1,0:T(8,128)(2,1)S(1)}, u32[]{:S(2)}, u32[]{:S(2)}) collective-permute-start(bf16[8,4,256,256]{3,2,1,0:T(8,128)(2,1)} %param.6), channel_id=1, source_target_pairs={{1,0},{2,1},{3,2},{4,3},{5,4},{6,5},{7,6},{9,8},{10,9},{11,10},{12... | collective-permute-start | bytes 12582920 | tf_op jit(solution)/shard_map/ppermute | solution.py:12
  102.4 2.0 copy-start
  105.8 54.6 %collective-permute-start.3 = (bf16[4,4,256,256]{3,2,1,0:T(8,128)(2,1)}, bf16[4,4,256,256]{3,2,1,0:T(8,128)(2,1)S(1)}, u32[]{:S(2)}, u32[]{:S(2)}) collective-permute-start(bf16[4,4,256,256]{3,2,1,0:T(8,128)(2,1)} %slice.12), channel_id=1, source_target_pairs={{1,0},{2,1},{3,2},{4,3},{5,4},{6,5},{7,6},{9,8},{10,9},{11,10},{12... | collective-permute-start | bytes 6291464 | tf_op jit(solution)/shard_map/ppermute | solution.py:12
  107.1 47.6 %collective-permute-start = (s32[8,4]{0,1:T(4,128)S(1)}, s32[8,4]{0,1:T(4,128)S(1)}, u32[]{:S(2)}, u32[]{:S(2)}) collective-permute-start(s32[8,4]{0,1:T(4,128)S(1)} %copy-done.1), channel_id=1, source_target_pairs={{1,0},{2,1},{3,2},{4,3},{5,4},{6,5},{7,6},{9,8},{10,9},{11,10},{12... | collective-permute-start | bytes 392 | tf_op jit(solution)/shard_map/ppermute | solution.py:12
  154.8 5.5 %collective-permute-start.1 = (s32[4,4]{0,1:T(4,128)S(1)}, s32[4,4]{0,1:T(4,128)S(1)}, u32[]{:S(2)}, u32[]{:S(2)}) collective-permute-start(s32[4,4]{0,1:T(4,128)S(1)} %bitcast.56), channel_id=1, source_target_pairs={{1,0},{2,1},{3,2},{4,3},{5,4},{6,5},{7,6},{9,8},{10,9},{11,10},{12... | collective-permute-start | bytes 200 | tf_op jit(solution)/shard_map/ppermute | solution.py:12
Sparse Core Ops, SparseCore 0:
  259.3 157.6 all-gather.2
